TPU v7x, 256 devices: a whole 4x4x8 slice. The times are simulated.
256 devices in a mesh: seq: 64 (over y, z, core), tp: 4 (over x).
Axes of the slice: x: 4, y: 4, z: 8, core: 2. Of those that a mesh axis runs over, the one named last changes fastest.
Arguments:
- tokens: bfloat16 [24576, 1024], P(('seq', 'tp')), may hold values from -6 to 6
- w_in: bfloat16 [3, 1024, 1024], P(None, None, 'tp'), may hold values from -0.1875 to 0.1875
- short_taps: float32 [3, 3, 1024], P(None, None, 'tp'), may hold values from -3.5 to 3.5
- skip_bias: float32 [2, 1024], P(None, 'tp'), may hold values from -4 to 4
- filter_spectra: float32 [2, 2, 128, 384, 1024], P(None, None, 'seq', None, 'tp'), may hold values from -6 to 6
- w_out: bfloat16 [1024, 1024], P('tp'), may hold values from -0.1875 to 0.1875
Outputs:
- mixed_out: bfloat16 [24576, 1024], P(('seq', 'tp'))
All inputs are finite; a program needn't handle non-finite values.
Results may differ from a plain program's by a relative error of at most 0.007.
Values may be sent and summed in bfloat16 or wider, within the bound.
A program may use at most 64 MiB of HBM per device.

v0:
```python
import math
import jax
import jax.numpy as jnp
from jax import lax
from jax.sharding import PartitionSpec as P

PRECISE = lax.Precision.HIGHEST


def passed_along(array, axis, by):
    length = lax.axis_size(axis)
    pairs = [(i, i + by) for i in range(length) if 0 <= i + by < length]
    return lax.ppermute(array, axis, pairs)


def phase_table(row_count, col_count, period, direction):
    row_index = jnp.arange(row_count, dtype=jnp.int32)[:, None]
    col_index = jnp.arange(col_count, dtype=jnp.int32)[None, :]
    phases = row_index * col_index % period
    angles = direction * 2.0 * math.pi / period * phases.astype(jnp.float32)
    return (jnp.cos(angles), jnp.sin(angles))


def conjugate(pair):
    return (pair[0], -pair[1])


def product(first_pair, second_pair):
    real_part = first_pair[0] * second_pair[0] - first_pair[1] * second_pair[1]
    imag_part = first_pair[0] * second_pair[1] + first_pair[1] * second_pair[0]
    return (real_part, imag_part)


def contract(pattern, table_pair, value_pair):
    real_part = jnp.einsum(pattern, table_pair[0], value_pair[0], precision=PRECISE) - jnp.einsum(
        pattern, table_pair[1], value_pair[1], precision=PRECISE
    )
    imag_part = jnp.einsum(pattern, table_pair[0], value_pair[1], precision=PRECISE) + jnp.einsum(
        pattern, table_pair[1], value_pair[0], precision=PRECISE
    )
    return (real_part, imag_part)


def local(tokens, w_in, short_taps, skip_bias, filter_spectra, w_out):
    seq_count = lax.axis_size("seq")
    device = lax.axis_index("seq")
    blocks = 2 * seq_count
    projected = jnp.einsum(
        "rd,sdc->src",
        lax.all_gather(tokens, "tp", axis=0, tiled=True),
        w_in,
        preferred_element_type=jnp.float32,
    ).astype(jnp.bfloat16)
    positions = projected.shape[1]
    channels = projected.shape[2]
    before = passed_along(projected[:, -2:, :], "seq", 1)
    extended = jnp.concatenate([before, projected], axis=1).astype(jnp.float32)
    filtered = (
        short_taps[:, 0, None, :] * extended[:, 2:]
        + short_taps[:, 1, None, :] * extended[:, 1:-1]
        + short_taps[:, 2, None, :] * extended[:, :-2]
    )
    factor_one = max(
        (factor for factor in range(1, math.isqrt(positions) + 1) if positions % factor == 0)
    )
    factor_two = positions // factor_one
    forward_pair = phase_table(blocks, seq_count, blocks, -1.0)
    inverse_pair = phase_table(seq_count, blocks, blocks, 1.0)
    outer_table = phase_table(factor_one, factor_one, factor_one, -1.0)
    inner_table = phase_table(factor_two, factor_two, factor_two, -1.0)
    twist_pair = phase_table(factor_one, factor_two, positions, -1.0)
    twist_pair = (twist_pair[0][None, :, :, None], twist_pair[1][None, :, :, None])
    freq_index = 2 * device + jnp.arange(2, dtype=jnp.int32)[:, None]
    pos_index = jnp.arange(positions, dtype=jnp.int32)[None, :]
    angles = -2.0 * math.pi / (blocks * positions) * (freq_index * pos_index).astype(jnp.float32)
    twiddle = (jnp.cos(angles)[:, :, None], jnp.sin(angles)[:, :, None])
    carried = filtered[0]
    for order_index in range(2):
        columns = lax.all_to_all(carried[None], "seq", split_axis=1, concat_axis=0, tiled=True)
        partial_re = jnp.einsum("kp,pqc->kqc", forward_pair[0], columns, precision=PRECISE)
        partial_im = jnp.einsum("kp,pqc->kqc", forward_pair[1], columns, precision=PRECISE)
        line_pair = (
            lax.all_to_all(partial_re, "seq", split_axis=0, concat_axis=1, tiled=True),
            lax.all_to_all(partial_im, "seq", split_axis=0, concat_axis=1, tiled=True),
        )
        line_pair = product(line_pair, twiddle)
        spectrum = tuple(
            (member.reshape(2, factor_one, factor_two, channels) for member in line_pair)
        )
        spectrum = contract("ca,jabk->jcbk", outer_table, spectrum)
        spectrum = product(spectrum, twist_pair)
        spectrum = contract("db,jcbk->jdck", inner_table, spectrum)
        response = (
            filter_spectra[order_index, 0].reshape(2, factor_two, factor_one, channels),
            filter_spectra[order_index, 1].reshape(2, factor_two, factor_one, channels),
        )
        spectrum = product(spectrum, response)
        spectrum = contract("db,jdck->jcbk", conjugate(inner_table), spectrum)
        spectrum = product(spectrum, conjugate(twist_pair))
        spectrum = contract("ca,jcbk->jabk", conjugate(outer_table), spectrum)
        line_pair = tuple(
            (member.reshape(2, positions, channels) / positions for member in spectrum)
        )
        line_pair = product(line_pair, conjugate(twiddle))
        real_rows = jnp.einsum(
            "pk,kqc->pqc",
            inverse_pair[0],
            lax.all_to_all(line_pair[0], "seq", split_axis=1, concat_axis=0, tiled=True),
            precision=PRECISE,
        ) - jnp.einsum(
            "pk,kqc->pqc",
            inverse_pair[1],
            lax.all_to_all(line_pair[1], "seq", split_axis=1, concat_axis=0, tiled=True),
            precision=PRECISE,
        )
        result = lax.all_to_all(real_rows / blocks, "seq", split_axis=0, concat_axis=1, tiled=True)[
            0
        ]
        carried = filtered[order_index + 1] * (result + skip_bias[order_index] * carried)
    gated_out = carried.astype(jnp.bfloat16)
    summed = lax.psum_scatter(
        jnp.dot(gated_out, w_out, preferred_element_type=jnp.float32),
        "tp",
        scatter_dimension=0,
        tiled=True,
    )
    return summed.astype(jnp.bfloat16)


def solution(mesh):
    in_specs = (
        P(("seq", "tp"), None),
        P(None, None, "tp"),
        P(None, None, "tp"),
        P(None, "tp"),
        P(None, None, "seq", None, "tp"),
        P("tp", None),
    )
    out_specs = P(("seq", "tp"), None)
    return jax.shard_map(local, mesh=mesh, in_specs=in_specs, out_specs=out_specs, check_vma=False)
```

profile of v0, /device:TPU:8, one launch (start us, length us, event | category | flops | bytes accessed | tf_op | source)
XLA Modules:
  0.0 486.5 jit_solution(2694065401096097672)
XLA Ops:
  6.5 14.0 %all_gather.3 = bf16[384,1024]{1,0:T(8,128)(2,1)S(1)} all-gather(bf16[96,1024]{1,0:T(8,128)(2,1)} %param.6), channel_id=1, replica_groups=mesh['seq'=64,'tp'=4] {'tp'}, dimensions={0}, use_global_device_ids=true | all-gather | bytes 983040 | tf_op jit(solution)/shard_map/all_gather | solution.py:50
  23.7 7.1 %collective-permute-done = bf16[3,2,256]{1,2,0:T(8,128)(2,1)S(1)} collective-permute-done((bf16[3,2,256]{1,2,0:T(8,128)(2,1)S(1)}, bf16[3,2,256]{1,2,0:T(8,128)(2,1)S(1)}, u32[]{:S(2)}, u32[]{:S(2)}) %collective-permute-start) | collective-permute-done | bytes 3104 | tf_op jit(solution)/shard_map/ppermute | solution.py:13
  32.8 25.1 %all_to_all.186 = f32[1,384,256]{2,0,1:T(1,128)S(1)} all-to-all(f32[1,384,256]{2,0,1:T(1,128)S(1)} %copy.211), channel_id=1, replica_groups=mesh['seq'=64,'tp'=4] {'seq'}, dimensions={1} | all-to-all | bytes 786432 | tf_op jit(solution)/shard_map/all_to_all | solution.py:79
  70.5 24.7 %all-to-all-done.2 = f32[128,6,256]{2,1,0:T(8,128)S(1)} async-done(((f32[128,6,256]{2,1,0:T(8,128)}), f32[128,6,256]{2,1,0:T(8,128)S(1)}, u32[]{:S(2)}, u32[]{:S(2)}) %all-to-all-start.2) | async-done | bytes 786464 | tf_op jit(solution)/shard_map/all_to_all | solution.py:84
  95.1 7.8 %all-to-all-start.1 = ((f32[128,6,256]{2,1,0:T(8,128)}), f32[128,6,256]{2,1,0:T(8,128)}, u32[]{:S(2)}, u32[]{:S(2)}) async-start(f32[128,6,256]{2,1,0:T(8,128)} %copy.213), calls=%async_computation.1 | async-start | bytes 2097152 | tf_op jit(solution)/shard_map/all_to_all | solution.py:83
  111.6 18.4 %all-to-all-done.1 = f32[128,6,256]{2,1,0:T(8,128)} async-done(((f32[128,6,256]{2,1,0:T(8,128)}), f32[128,6,256]{2,1,0:T(8,128)}, u32[]{:S(2)}, u32[]{:S(2)}) %all-to-all-start.1) | async-done | bytes 786464 | tf_op jit(solution)/shard_map/all_to_all | solution.py:83
  155.5 7.6 %all-to-all-start.3 = ((f32[2,384,256]{2,0,1:T(2,128)}), f32[2,384,256]{2,0,1:T(2,128)S(1)}, u32[]{:S(2)}, u32[]{:S(2)}) async-start(f32[2,384,256]{2,0,1:T(2,128)} %copy.248), calls=%async_computation.3 | async-start | bytes 1572864 | tf_op jit(solution)/shard_map/all_to_all | solution.py:108
  164.7 20.4 %all-to-all-done.3 = f32[2,384,256]{2,0,1:T(2,128)S(1)} async-done(((f32[2,384,256]{2,0,1:T(2,128)}), f32[2,384,256]{2,0,1:T(2,128)S(1)}, u32[]{:S(2)}, u32[]{:S(2)}) %all-to-all-start.3) | async-done | bytes 786464 | tf_op jit(solution)/shard_map/all_to_all | solution.py:108
  185.1 7.6 %all-to-all-start.4 = ((f32[2,384,256]{2,0,1:T(2,128)}), f32[2,384,256]{2,0,1:T(2,128)S(1)}, u32[]{:S(2)}, u32[]{:S(2)}) async-start(f32[2,384,256]{2,0,1:T(2,128)} %copy.250), calls=%async_computation.4 | async-start | bytes 1572864 | tf_op jit(solution)/shard_map/all_to_all | solution.py:113
  194.9 19.5 %all-to-all-done.4 = f32[2,384,256]{2,0,1:T(2,128)S(1)} async-done(((f32[2,384,256]{2,0,1:T(2,128)}), f32[2,384,256]{2,0,1:T(2,128)S(1)}, u32[]{:S(2)}, u32[]{:S(2)}) %all-to-all-start.4) | async-done | bytes 786464 | tf_op jit(solution)/shard_map/all_to_all | solution.py:113
  217.4 7.3 %all-to-all-start.5 = ((f32[64,6,256]{2,1,0:T(8,128)}), f32[64,6,256]{2,1,0:T(8,128)S(1)}, u32[]{:S(2)}, u32[]{:S(2)}) async-start(f32[64,6,256]{2,1,0:T(8,128)} %copy.252), calls=%async_computation.5 | async-start | bytes 1048576 | tf_op jit(solution)/shard_map/all_to_all | solution.py:116
  225.3 16.1 %all-to-all-done.5 = f32[64,6,256]{2,1,0:T(8,128)S(1)} async-done(((f32[64,6,256]{2,1,0:T(8,128)}), f32[64,6,256]{2,1,0:T(8,128)S(1)}, u32[]{:S(2)}, u32[]{:S(2)}) %all-to-all-start.5) | async-done | bytes 393248 | tf_op jit(solution)/shard_map/all_to_all | solution.py:116
  242.3 20.8 %all_to_all.187 = f32[1,384,256]{2,0,1:T(1,128)S(1)} all-to-all(f32[1,384,256]{2,0,1:T(1,128)S(1)} %copy.254), channel_id=1, replica_groups=mesh['seq'=64,'tp'=4] {'seq'}, dimensions={1} | all-to-all | bytes 786432 | tf_op jit(solution)/shard_map/all_to_all | solution.py:79
  266.5 6.7 %all-to-all-start.7 = ((f32[128,6,256]{2,1,0:T(8,128)}), f32[128,6,256]{2,1,0:T(8,128)S(1)}, u32[]{:S(2)}, u32[]{:S(2)}) async-start(f32[128,6,256]{2,1,0:T(8,128)} %copy.256), calls=%async_computation.7 | async-start | bytes 2097152 | tf_op jit(solution)/shard_map/all_to_all | solution.py:83
  275.7 24.7 %all-to-all-done.7 = f32[128,6,256]{2,1,0:T(8,128)S(1)} async-done(((f32[128,6,256]{2,1,0:T(8,128)}), f32[128,6,256]{2,1,0:T(8,128)S(1)}, u32[]{:S(2)}, u32[]{:S(2)}) %all-to-all-start.7) | async-done | bytes 786464 | tf_op jit(solution)/shard_map/all_to_all | solution.py:83
  300.4 7.8 %all-to-all-start.8 = ((f32[128,6,256]{2,1,0:T(8,128)}), f32[128,6,256]{2,1,0:T(8,128)}, u32[]{:S(2)}, u32[]{:S(2)}) async-start(f32[128,6,256]{2,1,0:T(8,128)} %copy.259), calls=%async_computation.8 | async-start | bytes 2097152 | tf_op jit(solution)/shard_map/all_to_all | solution.py:84
  308.6 26.6 %all-to-all-done.8 = f32[128,6,256]{2,1,0:T(8,128)} async-done(((f32[128,6,256]{2,1,0:T(8,128)}), f32[128,6,256]{2,1,0:T(8,128)}, u32[]{:S(2)}, u32[]{:S(2)}) %all-to-all-start.8) | async-done | bytes 786464 | tf_op jit(solution)/shard_map/all_to_all | solution.py:84
  360.9 7.6 %all-to-all-start.9 = ((f32[2,384,256]{2,0,1:T(2,128)}), f32[2,384,256]{2,0,1:T(2,128)S(1)}, u32[]{:S(2)}, u32[]{:S(2)}) async-start(f32[2,384,256]{2,0,1:T(2,128)} %copy.287), calls=%async_computation.9 | async-start | bytes 1572864 | tf_op jit(solution)/shard_map/all_to_all | solution.py:108
  370.0 20.4 %all-to-all-done.9 = f32[2,384,256]{2,0,1:T(2,128)S(1)} async-done(((f32[2,384,256]{2,0,1:T(2,128)}), f32[2,384,256]{2,0,1:T(2,128)S(1)}, u32[]{:S(2)}, u32[]{:S(2)}) %all-to-all-start.9) | async-done | bytes 786464 | tf_op jit(solution)/shard_map/all_to_all | solution.py:108
  390.3 7.6 %all-to-all-start.10 = ((f32[2,384,256]{2,0,1:T(2,128)}), f32[2,384,256]{2,0,1:T(2,128)S(1)}, u32[]{:S(2)}, u32[]{:S(2)}) async-start(f32[2,384,256]{2,0,1:T(2,128)} %copy.289), calls=%async_computation.10 | async-start | bytes 1572864 | tf_op jit(solution)/shard_map/all_to_all | solution.py:113
  402.2 17.5 %all-to-all-done.10 = f32[2,384,256]{2,0,1:T(2,128)S(1)} async-done(((f32[2,384,256]{2,0,1:T(2,128)}), f32[2,384,256]{2,0,1:T(2,128)S(1)}, u32[]{:S(2)}, u32[]{:S(2)}) %all-to-all-start.10) | async-done | bytes 786464 | tf_op jit(solution)/shard_map/all_to_all | solution.py:113
  424.3 7.3 %all-to-all-start.11 = ((f32[64,6,256]{2,1,0:T(8,128)}), f32[64,6,256]{2,1,0:T(8,128)S(1)}, u32[]{:S(2)}, u32[]{:S(2)}) async-start(f32[64,6,256]{2,1,0:T(8,128)} %copy.291), calls=%async_computation.11 | async-start | bytes 1048576 | tf_op jit(solution)/shard_map/all_to_all | solution.py:116
  432.0 16.4 %all-to-all-done.11 = f32[64,6,256]{2,1,0:T(8,128)S(1)} async-done(((f32[64,6,256]{2,1,0:T(8,128)}), f32[64,6,256]{2,1,0:T(8,128)S(1)}, u32[]{:S(2)}, u32[]{:S(2)}) %all-to-all-start.11) | async-done | bytes 393248 | tf_op jit(solution)/shard_map/all_to_all | solution.py:116
  451.5 26.2 %reduce-scatter.2.cloned.1.call-done = f32[96,1024]{1,0:T(8,128)} async-done(((f32[384,1024]{1,0:T(8,128)}), f32[96,1024]{1,0:T(8,128)}) %reduce-scatter.2.cloned.1.call-update) | async-done | bytes 393232 | tf_op jit(solution)/shard_map/reduce_scatter | solution.py:121
  (159 shorter events, 106.7 us)
Async XLA Ops:
  6.5 14.0 %copy-start = (bf16[3,1024,256]{2,1,0:T(8,128)(2,1)S(1)}, bf16[3,1024,256]{2,1,0:T(8,128)(2,1)}, u32[]{:S(2)}) copy-start(bf16[3,1024,256]{2,1,0:T(8,128)(2,1)} %param.7) | copy-start | bytes 4718596
  20.5 3.1 copy-start.22
  21.7 9.1 %collective-permute-start = (bf16[3,2,256]{1,2,0:T(8,128)(2,1)S(1)}, bf16[3,2,256]{1,2,0:T(8,128)(2,1)S(1)}, u32[]{:S(2)}, u32[]{:S(2)}) collective-permute-start(bf16[3,2,256]{1,2,0:T(8,128)(2,1)S(1)} %slice.64), channel_id=1, source_target_pairs={{0,4},{4,8},{8,12},{12,16},{16,20},{20,24},{24,28},{28,32},{32,36}... | collective-permute-start | bytes 9224 | tf_op jit(solution)/shard_map/ppermute | solution.py:13
  61.3 33.8 %all-to-all-start.2 = ((f32[128,6,256]{2,1,0:T(8,128)}), f32[128,6,256]{2,1,0:T(8,128)S(1)}, u32[]{:S(2)}, u32[]{:S(2)}) async-start(f32[128,6,256]{2,1,0:T(8,128)} %copy.217), calls=%async_computation.2 | async-start | bytes 2097152 | tf_op jit(solution)/shard_map/all_to_all | solution.py:84
  95.1 34.9 %all-to-all-start.1 = ((f32[128,6,256]{2,1,0:T(8,128)}), f32[128,6,256]{2,1,0:T(8,128)}, u32[]{:S(2)}, u32[]{:S(2)}) async-start(f32[128,6,256]{2,1,0:T(8,128)} %copy.213), calls=%async_computation.1 | async-start | bytes 2097152 | tf_op jit(solution)/shard_map/all_to_all | solution.py:83
  130.0 1.7 copy-start.6
  130.0 1.7 copy-start.8
  155.5 29.5 %all-to-all-start.3 = ((f32[2,384,256]{2,0,1:T(2,128)}), f32[2,384,256]{2,0,1:T(2,128)S(1)}, u32[]{:S(2)}, u32[]{:S(2)}) async-start(f32[2,384,256]{2,0,1:T(2,128)} %copy.248), calls=%async_computation.3 | async-start | bytes 1572864 | tf_op jit(solution)/shard_map/all_to_all | solution.py:108
  185.1 29.3 %all-to-all-start.4 = ((f32[2,384,256]{2,0,1:T(2,128)}), f32[2,384,256]{2,0,1:T(2,128)S(1)}, u32[]{:S(2)}, u32[]{:S(2)}) async-start(f32[2,384,256]{2,0,1:T(2,128)} %copy.250), calls=%async_computation.4 | async-start | bytes 1572864 | tf_op jit(solution)/shard_map/all_to_all | solution.py:113
  216.3 8.4 %copy-start.24 = (f32[2,256]{1,0:T(2,128)S(1)}, f32[2,256]{1,0:T(2,128)}, u32[]{:S(2)}) copy-start(f32[2,256]{1,0:T(2,128)} %param.9) | copy-start | bytes 6148
  217.4 24.0 %all-to-all-start.5 = ((f32[64,6,256]{2,1,0:T(8,128)}), f32[64,6,256]{2,1,0:T(8,128)S(1)}, u32[]{:S(2)}, u32[]{:S(2)}) async-start(f32[64,6,256]{2,1,0:T(8,128)} %copy.252), calls=%async_computation.5 | async-start | bytes 1048576 | tf_op jit(solution)/shard_map/all_to_all | solution.py:116
  225.3 16.5 %copy-start.20 = (f32[1,256]{1,0:T(1,128)}, f32[1,256]{1,0:T(1,128)S(1)}, u32[]{:S(2)}) copy-start(f32[1,256]{1,0:T(1,128)S(1)} %get-tuple-element.35) | copy-start | bytes 3076
  266.5 33.9 %all-to-all-start.7 = ((f32[128,6,256]{2,1,0:T(8,128)}), f32[128,6,256]{2,1,0:T(8,128)S(1)}, u32[]{:S(2)}, u32[]{:S(2)}) async-start(f32[128,6,256]{2,1,0:T(8,128)} %copy.256), calls=%async_computation.7 | async-start | bytes 2097152 | tf_op jit(solution)/shard_map/all_to_all | solution.py:83
  300.4 34.9 %all-to-all-start.8 = ((f32[128,6,256]{2,1,0:T(8,128)}), f32[128,6,256]{2,1,0:T(8,128)}, u32[]{:S(2)}, u32[]{:S(2)}) async-start(f32[128,6,256]{2,1,0:T(8,128)} %copy.259), calls=%async_computation.8 | async-start | bytes 2097152 | tf_op jit(solution)/shard_map/all_to_all | solution.py:84
  308.6 28.3 %copy-start.7 = (f32[2,16,24]{0,2,1:T(8,128)S(1)}, f32[2,16,24]{0,2,1:T(8,128)}, u32[]{:S(2)}) copy-start(f32[2,16,24]{0,2,1:T(8,128)} %copy.215) | copy-start | bytes 9220
  335.2 1.7 copy-start.9
  360.9 29.5 %all-to-all-start.9 = ((f32[2,384,256]{2,0,1:T(2,128)}), f32[2,384,256]{2,0,1:T(2,128)S(1)}, u32[]{:S(2)}, u32[]{:S(2)}) async-start(f32[2,384,256]{2,0,1:T(2,128)} %copy.287), calls=%async_computation.9 | async-start | bytes 1572864 | tf_op jit(solution)/shard_map/all_to_all | solution.py:108
  390.3 29.4 %all-to-all-start.10 = ((f32[2,384,256]{2,0,1:T(2,128)}), f32[2,384,256]{2,0,1:T(2,128)S(1)}, u32[]{:S(2)}, u32[]{:S(2)}) async-start(f32[2,384,256]{2,0,1:T(2,128)} %copy.289), calls=%async_computation.10 | async-start | bytes 1572864 | tf_op jit(solution)/shard_map/all_to_all | solution.py:113
  420.9 1.7 copy-start.11
  424.3 24.0 %all-to-all-start.11 = ((f32[64,6,256]{2,1,0:T(8,128)}), f32[64,6,256]{2,1,0:T(8,128)S(1)}, u32[]{:S(2)}, u32[]{:S(2)}) async-start(f32[64,6,256]{2,1,0:T(8,128)} %copy.291), calls=%async_computation.11 | async-start | bytes 1048576 | tf_op jit(solution)/shard_map/all_to_all | solution.py:116
  431.7 46.1 %reduce-scatter.2.cloned.1.call-start = ((), (), s32[]{:S(2)}) async-start(), calls=%async_computation.13 | async-start | bytes 1966080 | tf_op jit(solution)/shard_map/reduce_scatter | solution.py:121
  431.8 16.8 %copy-start.21 = (f32[1,256]{1,0:T(1,128)S(1)}, f32[1,256]{1,0:T(1,128)}, u32[]{:S(2)}) copy-start(f32[1,256]{1,0:T(1,128)} %copy-done.20) | copy-start | bytes 3076
  431.8 16.8 %copy-start.23 = (f32[1,256]{1,0:T(1,128)S(1)}, f32[1,256]{1,0:T(1,128)}, u32[]{:S(2)}) copy-start(f32[1,256]{1,0:T(1,128)} %get-tuple-element.34) | copy-start | bytes 3076
  448.6 30.8 %copy-start.1 = (bf16[3,1024,256]{2,1,0:T(8,128)(2,1)S(1)}, bf16[3,1024,256]{2,1,0:T(8,128)(2,1)}, u32[]{:S(2)}) copy-start(bf16[3,1024,256]{2,1,0:T(8,128)(2,1)} %param.7) | copy-start | bytes 4718596
  (13 other events, 13.9 us)
Sparse Core Ops, SparseCore 0:
  451.6 26.0 reduce-scatter.1
where the time goes:
time: 496 us; the launch traced here: 487 us
  waiting for transfers between devices  238 us (48%)
  starting transfers between devices  76.1 us (15%)
  blocking collectives  59.9 us (12%)
  matrix products  50.6 us (10%)
  local copies, waits for them, and re-layouts  37.5 us (8%)
  between operations  14.6 us (3%)
  other arithmetic  9.98 us (2%)
    all_to_all x2, waiting for transfers between devices, local(): lax.all_to_all(partial_im, 'seq', split_axis=0, concat_axis=1, tiled=True)  51.3 us
    all_to_all x2, blocking collectives, local(): lax.all_to_all(carried[None], 'seq', split_axis=1, concat_axis=0, tiled=T...  45.9 us
    all_to_all x2, waiting for transfers between devices, local(): lax.all_to_all(partial_re, 'seq', split_axis=0, concat_axis=1, tiled=True)  43 us
    all_to_all x2, waiting for transfers between devices, local(): lax.all_to_all(line_pair[0], 'seq', split_axis=1, concat_axis=0, tiled=True)  40.7 us
    all_to_all x2, waiting for transfers between devices, local(): lax.all_to_all(line_pair[1], 'seq', split_axis=1, concat_axis=0, tiled=True)  37 us
    all_to_all x2, waiting for transfers between devices, local(): lax.all_to_all(real_rows / blocks, 'seq', split_axis=0, concat_axis=1, ti...  32.5 us
    reduce_scatter x1, waiting for transfers between devices, local(): lax.psum_scatter(jnp.dot(gated_out, w_out, preferred_element_type=jnp.flo...  26.2 us
    all_to_all x2, starting transfers between devices, local(): lax.all_to_all(line_pair[0], 'seq', split_axis=1, concat_axis=0, tiled=True)  15.2 us
  transfers between devices with their start and end apart: 12, of which 12 were waited for; matrix products, arithmetic and copies ran while one was open for 5% of the time, Pallas kernels for 0%

commit v1 on v0

--- a/solution.py
+++ b/solution.py
@@ -76,7 +76,12 @@
     twiddle = (jnp.cos(angles)[:, :, None], jnp.sin(angles)[:, :, None])
     carried = filtered[0]
     for order_index in range(2):
-        columns = lax.all_to_all(carried[None], "seq", split_axis=1, concat_axis=0, tiled=True)
+        columns = jnp.concatenate(
+            lax.all_to_all(
+                jnp.stack(jnp.split(carried[None], lax.axis_size("seq"), axis=1)), "seq", 0, 0
+            ),
+            axis=0,
+        )
         partial_re = jnp.einsum("kp,pqc->kqc", forward_pair[0], columns, precision=PRECISE)
         partial_im = jnp.einsum("kp,pqc->kqc", forward_pair[1], columns, precision=PRECISE)
         line_pair = (

time: 496 us -> 609 us (1.23)
  local copies, waits for them, and re-layouts: 37.5 us -> 151 us
  waiting for transfers between devices: 238 us -> 231 us
    unnamed x52 -> x162, local copies, waits for them, and re-layouts: 1.06 us -> 94.4 us
    another operation x0 -> x4, local copies, waits for them, and re-layouts: none -> 12 us  [local(): jnp.stack(jnp.split(carried[None], lax.axis_size('seq'), axis=1))]
    all_to_all x2, waiting for transfers between devices: 51.3 us -> 44.1 us  [local(): lax.all_to_all(partial_im, 'seq', split_axis=0, concat_axis=1, tiled=True)]
    all_to_all x2, waiting for transfers between devices: 43 us -> 49.4 us  [local(): lax.all_to_all(partial_re, 'seq', split_axis=0, concat_axis=1, tiled=True)]
where the time goes in v1:
time: 609 us; the launch traced here: 598 us
  waiting for transfers between devices  231 us (38%)
  local copies, waits for them, and re-layouts  151 us (25%)
  starting transfers between devices  76.8 us (13%)
  blocking collectives  60.1 us (10%)
  matrix products  54.3 us (9%)
  between operations  14.7 us (2%)
  other arithmetic  10.6 us (2%)
    unnamed x162, local copies, waits for them, and re-layouts  94.4 us
    all_to_all x2, waiting for transfers between devices, local(): lax.all_to_all(partial_re, 'seq', split_axis=0, concat_axis=1, tiled=True)  49.4 us
    all_to_all x2, blocking collectives, local(): lax.all_to_all(jnp.stack(jnp.split(carried[None], lax.axis_size('seq'), a...  46.1 us
    all_to_all x2, waiting for transfers between devices, local(): lax.all_to_all(partial_im, 'seq', split_axis=0, concat_axis=1, tiled=True)  44.1 us
    all_to_all x2, waiting for transfers between devices, local(): lax.all_to_all(line_pair[0], 'seq', split_axis=1, concat_axis=0, tiled=True)  40.7 us
    all_to_all x2, waiting for transfers between devices, local(): lax.all_to_all(line_pair[1], 'seq', split_axis=1, concat_axis=0, tiled=True)  34.7 us
    all_to_all x2, waiting for transfers between devices, local(): lax.all_to_all(real_rows / blocks, 'seq', split_axis=0, concat_axis=1, ti...  29.9 us
    reduce_scatter x1, waiting for transfers between devices, local(): lax.psum_scatter(jnp.dot(gated_out, w_out, preferred_element_type=jnp.flo...  26.2 us
  transfers between devices with their start and end apart: 12, of which 12 were waited for; matrix products, arithmetic and copies ran while one was open for 5% of the time, Pallas kernels for 0%

profile of v1, /device:TPU:8, one launch (start us, length us, event | category | flops | bytes accessed | tf_op | source)
XLA Modules:
  0.0 598.4 jit_solution(12815051890196108458)
XLA Ops:
  6.5 14.0 %all_gather.3 = bf16[384,1024]{1,0:T(8,128)(2,1)S(1)} all-gather(bf16[96,1024]{1,0:T(8,128)(2,1)} %param.6), channel_id=1, replica_groups=mesh['seq'=64,'tp'=4] {'tp'}, dimensions={0}, use_global_device_ids=true | all-gather | bytes 983040 | tf_op jit(solution)/shard_map/all_gather | solution.py:50
  85.4 25.1 %all_to_all.172 = f32[64,1,6,256]{3,1,2,0:T(1,128)S(1)} all-to-all(f32[64,1,6,256]{3,1,2,0:T(1,128)S(1)} %copy.415), channel_id=1, replica_groups=mesh['seq'=64,'tp'=4] {'seq'}, dimensions={0} | all-to-all | bytes 786432 | tf_op jit(solution)/shard_map/all_to_all | solution.py:80
  112.9 6.7 %all-to-all-start.1 = ((f32[128,6,256]{2,1,0:T(8,128)}), f32[128,6,256]{2,1,0:T(8,128)S(1)}, u32[]{:S(2)}, u32[]{:S(2)}) async-start(f32[128,6,256]{2,1,0:T(8,128)} %copy.417), calls=%async_computation.1 | async-start | bytes 2097152 | tf_op jit(solution)/shard_map/all_to_all | solution.py:88
  122.1 24.7 %all-to-all-done.1 = f32[128,6,256]{2,1,0:T(8,128)S(1)} async-done(((f32[128,6,256]{2,1,0:T(8,128)}), f32[128,6,256]{2,1,0:T(8,128)S(1)}, u32[]{:S(2)}, u32[]{:S(2)}) %all-to-all-start.1) | async-done | bytes 786464 | tf_op jit(solution)/shard_map/all_to_all | solution.py:88
  146.8 7.8 %all-to-all-start.2 = ((f32[128,6,256]{2,1,0:T(8,128)}), f32[128,6,256]{2,1,0:T(8,128)}, u32[]{:S(2)}, u32[]{:S(2)}) async-start(f32[128,6,256]{2,1,0:T(8,128)} %copy.420), calls=%async_computation.2 | async-start | bytes 2097152 | tf_op jit(solution)/shard_map/all_to_all | solution.py:89
  163.3 18.4 %all-to-all-done.2 = f32[128,6,256]{2,1,0:T(8,128)} async-done(((f32[128,6,256]{2,1,0:T(8,128)}), f32[128,6,256]{2,1,0:T(8,128)}, u32[]{:S(2)}, u32[]{:S(2)}) %all-to-all-start.2) | async-done | bytes 786464 | tf_op jit(solution)/shard_map/all_to_all | solution.py:89
  209.0 7.6 %all-to-all-start.3 = ((f32[2,384,256]{2,0,1:T(2,128)}), f32[2,384,256]{2,0,1:T(2,128)S(1)}, u32[]{:S(2)}, u32[]{:S(2)}) async-start(f32[2,384,256]{2,0,1:T(2,128)} %copy.451), calls=%async_computation.3 | async-start | bytes 1572864 | tf_op jit(solution)/shard_map/all_to_all | solution.py:113
  218.1 20.4 %all-to-all-done.3 = f32[2,384,256]{2,0,1:T(2,128)S(1)} async-done(((f32[2,384,256]{2,0,1:T(2,128)}), f32[2,384,256]{2,0,1:T(2,128)S(1)}, u32[]{:S(2)}, u32[]{:S(2)}) %all-to-all-start.3) | async-done | bytes 786464 | tf_op jit(solution)/shard_map/all_to_all | solution.py:113
  238.5 7.8 %all-to-all-start.4 = ((f32[2,384,256]{2,0,1:T(2,128)}), f32[2,384,256]{2,0,1:T(2,128)S(1)}, u32[]{:S(2)}, u32[]{:S(2)}) async-start(f32[2,384,256]{2,0,1:T(2,128)} %copy.453), calls=%async_computation.4 | async-start | bytes 1572864 | tf_op jit(solution)/shard_map/all_to_all | solution.py:118
  248.6 19.5 %all-to-all-done.4 = f32[2,384,256]{2,0,1:T(2,128)S(1)} async-done(((f32[2,384,256]{2,0,1:T(2,128)}), f32[2,384,256]{2,0,1:T(2,128)S(1)}, u32[]{:S(2)}, u32[]{:S(2)}) %all-to-all-start.4) | async-done | bytes 786464 | tf_op jit(solution)/shard_map/all_to_all | solution.py:118
  271.6 7.3 %all-to-all-start.5 = ((f32[64,6,256]{2,1,0:T(8,128)}), f32[64,6,256]{2,1,0:T(8,128)S(1)}, u32[]{:S(2)}, u32[]{:S(2)}) async-start(f32[64,6,256]{2,1,0:T(8,128)} %copy.455), calls=%async_computation.5 | async-start | bytes 1048576 | tf_op jit(solution)/shard_map/all_to_all | solution.py:121
  280.2 15.4 %all-to-all-done.5 = f32[64,6,256]{2,1,0:T(8,128)S(1)} async-done(((f32[64,6,256]{2,1,0:T(8,128)}), f32[64,6,256]{2,1,0:T(8,128)S(1)}, u32[]{:S(2)}, u32[]{:S(2)}) %all-to-all-start.5) | async-done | bytes 393248 | tf_op jit(solution)/shard_map/all_to_all | solution.py:121
  349.1 20.9 %all_to_all.173 = f32[64,1,6,256]{3,1,2,0:T(1,128)S(1)} all-to-all(f32[64,1,6,256]{3,1,2,0:T(1,128)S(1)} %copy.457), channel_id=1, replica_groups=mesh['seq'=64,'tp'=4] {'seq'}, dimensions={0} | all-to-all | bytes 786432 | tf_op jit(solution)/shard_map/all_to_all | solution.py:80
  372.5 6.7 %all-to-all-start.7 = ((f32[128,6,256]{2,1,0:T(8,128)}), f32[128,6,256]{2,1,0:T(8,128)S(1)}, u32[]{:S(2)}, u32[]{:S(2)}) async-start(f32[128,6,256]{2,1,0:T(8,128)} %copy.459), calls=%async_computation.7 | async-start | bytes 2097152 | tf_op jit(solution)/shard_map/all_to_all | solution.py:88
  381.7 24.7 %all-to-all-done.7 = f32[128,6,256]{2,1,0:T(8,128)S(1)} async-done(((f32[128,6,256]{2,1,0:T(8,128)}), f32[128,6,256]{2,1,0:T(8,128)S(1)}, u32[]{:S(2)}, u32[]{:S(2)}) %all-to-all-start.7) | async-done | bytes 786464 | tf_op jit(solution)/shard_map/all_to_all | solution.py:88
  406.3 7.8 %all-to-all-start.8 = ((f32[128,6,256]{2,1,0:T(8,128)}), f32[128,6,256]{2,1,0:T(8,128)}, u32[]{:S(2)}, u32[]{:S(2)}) async-start(f32[128,6,256]{2,1,0:T(8,128)} %copy.461), calls=%async_computation.8 | async-start | bytes 2097152 | tf_op jit(solution)/shard_map/all_to_all | solution.py:89
  415.4 25.8 %all-to-all-done.8 = f32[128,6,256]{2,1,0:T(8,128)} async-done(((f32[128,6,256]{2,1,0:T(8,128)}), f32[128,6,256]{2,1,0:T(8,128)}, u32[]{:S(2)}, u32[]{:S(2)}) %all-to-all-start.8) | async-done | bytes 786464 | tf_op jit(solution)/shard_map/all_to_all | solution.py:89
  467.3 7.6 %all-to-all-start.9 = ((f32[2,384,256]{2,0,1:T(2,128)}), f32[2,384,256]{2,0,1:T(2,128)S(1)}, u32[]{:S(2)}, u32[]{:S(2)}) async-start(f32[2,384,256]{2,0,1:T(2,128)} %copy.489), calls=%async_computation.9 | async-start | bytes 1572864 | tf_op jit(solution)/shard_map/all_to_all | solution.py:113
  476.5 20.4 %all-to-all-done.9 = f32[2,384,256]{2,0,1:T(2,128)S(1)} async-done(((f32[2,384,256]{2,0,1:T(2,128)}), f32[2,384,256]{2,0,1:T(2,128)S(1)}, u32[]{:S(2)}, u32[]{:S(2)}) %all-to-all-start.9) | async-done | bytes 786464 | tf_op jit(solution)/shard_map/all_to_all | solution.py:113
  496.8 7.9 %all-to-all-start.10 = ((f32[2,384,256]{2,0,1:T(2,128)}), f32[2,384,256]{2,0,1:T(2,128)}, u32[]{:S(2)}, u32[]{:S(2)}) async-start(f32[2,384,256]{2,0,1:T(2,128)} %copy.491), calls=%async_computation.10 | async-start | bytes 1572864 | tf_op jit(solution)/shard_map/all_to_all | solution.py:118
  511.1 15.2 %all-to-all-done.10 = f32[2,384,256]{2,0,1:T(2,128)} async-done(((f32[2,384,256]{2,0,1:T(2,128)}), f32[2,384,256]{2,0,1:T(2,128)}, u32[]{:S(2)}, u32[]{:S(2)}) %all-to-all-start.10) | async-done | bytes 786464 | tf_op jit(solution)/shard_map/all_to_all | solution.py:118
  534.2 7.5 %all-to-all-start.11 = ((f32[64,6,256]{2,1,0:T(8,128)}), f32[64,6,256]{2,1,0:T(8,128)}, u32[]{:S(2)}, u32[]{:S(2)}) async-start(f32[64,6,256]{2,1,0:T(8,128)} %copy.493), calls=%async_computation.11 | async-start | bytes 1048576 | tf_op jit(solution)/shard_map/all_to_all | solution.py:121
  543.7 14.6 %all-to-all-done.11 = f32[64,6,256]{2,1,0:T(8,128)} async-done(((f32[64,6,256]{2,1,0:T(8,128)}), f32[64,6,256]{2,1,0:T(8,128)}, u32[]{:S(2)}, u32[]{:S(2)}) %all-to-all-start.11) | async-done | bytes 393248 | tf_op jit(solution)/shard_map/all_to_all | solution.py:121
  563.2 26.2 %reduce-scatter.2.cloned.1.call-done = f32[96,1024]{1,0:T(8,128)} async-done(((f32[384,1024]{1,0:T(8,128)}), f32[96,1024]{1,0:T(8,128)}) %reduce-scatter.2.cloned.1.call-update) | async-done | bytes 393232 | tf_op jit(solution)/shard_map/reduce_scatter | solution.py:126
  (266 shorter events, 223.8 us)
Async XLA Ops:
  6.5 14.0 %copy-start = (bf16[3,1024,256]{2,1,0:T(8,128)(2,1)S(1)}, bf16[3,1024,256]{2,1,0:T(8,128)(2,1)}, u32[]{:S(2)}) copy-start(bf16[3,1024,256]{2,1,0:T(8,128)(2,1)} %param.7) | copy-start | bytes 4718596
  21.7 9.1 %collective-permute-start = (bf16[3,2,256]{1,2,0:T(8,128)(2,1)S(1)}, bf16[3,2,256]{1,2,0:T(8,128)(2,1)S(1)}, u32[]{:S(2)}, u32[]{:S(2)}) collective-permute-start(bf16[3,2,256]{1,2,0:T(8,128)(2,1)S(1)} %slice.128), channel_id=1, source_target_pairs={{0,4},{4,8},{8,12},{12,16},{16,20},{20,24},{24,28},{28,32},{32,36}... | collective-permute-start | bytes 9224 | tf_op jit(solution)/shard_map/ppermute | solution.py:13
  112.9 33.8 %all-to-all-start.1 = ((f32[128,6,256]{2,1,0:T(8,128)}), f32[128,6,256]{2,1,0:T(8,128)S(1)}, u32[]{:S(2)}, u32[]{:S(2)}) async-start(f32[128,6,256]{2,1,0:T(8,128)} %copy.417), calls=%async_computation.1 | async-start | bytes 2097152 | tf_op jit(solution)/shard_map/all_to_all | solution.py:88
  146.8 34.9 %all-to-all-start.2 = ((f32[128,6,256]{2,1,0:T(8,128)}), f32[128,6,256]{2,1,0:T(8,128)}, u32[]{:S(2)}, u32[]{:S(2)}) async-start(f32[128,6,256]{2,1,0:T(8,128)} %copy.420), calls=%async_computation.2 | async-start | bytes 2097152 | tf_op jit(solution)/shard_map/all_to_all | solution.py:89
  183.3 12.9 %copy-start.4 = (f32[1,1,2,384,256]{4,3,2,1,0:T(8,128)S(1)}, f32[1,1,2,384,256]{4,3,2,1,0:T(8,128)}, u32[]{:S(2)}) copy-start(f32[1,1,2,384,256]{4,3,2,1,0:T(8,128)} %get-tuple-element.8) | copy-start | bytes 2359300
  183.3 12.9 %copy-start.5 = (f32[1,1,2,384,256]{4,3,2,1,0:T(8,128)S(1)}, f32[1,1,2,384,256]{4,3,2,1,0:T(8,128)}, u32[]{:S(2)}) copy-start(f32[1,1,2,384,256]{4,3,2,1,0:T(8,128)} %get-tuple-element.9) | copy-start | bytes 2359300
  209.0 29.5 %all-to-all-start.3 = ((f32[2,384,256]{2,0,1:T(2,128)}), f32[2,384,256]{2,0,1:T(2,128)S(1)}, u32[]{:S(2)}, u32[]{:S(2)}) async-start(f32[2,384,256]{2,0,1:T(2,128)} %copy.451), calls=%async_computation.3 | async-start | bytes 1572864 | tf_op jit(solution)/shard_map/all_to_all | solution.py:113
  238.5 29.6 %all-to-all-start.4 = ((f32[2,384,256]{2,0,1:T(2,128)}), f32[2,384,256]{2,0,1:T(2,128)S(1)}, u32[]{:S(2)}, u32[]{:S(2)}) async-start(f32[2,384,256]{2,0,1:T(2,128)} %copy.453), calls=%async_computation.4 | async-start | bytes 1572864 | tf_op jit(solution)/shard_map/all_to_all | solution.py:118
  271.6 24.0 %all-to-all-start.5 = ((f32[64,6,256]{2,1,0:T(8,128)}), f32[64,6,256]{2,1,0:T(8,128)S(1)}, u32[]{:S(2)}, u32[]{:S(2)}) async-start(f32[64,6,256]{2,1,0:T(8,128)} %copy.455), calls=%async_computation.5 | async-start | bytes 1048576 | tf_op jit(solution)/shard_map/all_to_all | solution.py:121
  280.2 54.7 %copy-start.14 = (f32[1,256]{1,0:T(1,128)}, f32[1,256]{1,0:T(1,128)S(1)}, u32[]{:S(2)}) copy-start(f32[1,256]{1,0:T(1,128)S(1)} %get-tuple-element.35) | copy-start | bytes 3076
  349.1 93.7 %copy-start.6 = (f32[2,16,24]{0,2,1:T(8,128)S(1)}, f32[2,16,24]{0,2,1:T(8,128)}, u32[]{:S(2)}) copy-start(f32[2,16,24]{0,2,1:T(8,128)} %copy.419) | copy-start | bytes 9220
  372.5 33.8 %all-to-all-start.7 = ((f32[128,6,256]{2,1,0:T(8,128)}), f32[128,6,256]{2,1,0:T(8,128)S(1)}, u32[]{:S(2)}, u32[]{:S(2)}) async-start(f32[128,6,256]{2,1,0:T(8,128)} %copy.459), calls=%async_computation.7 | async-start | bytes 2097152 | tf_op jit(solution)/shard_map/all_to_all | solution.py:88
  380.2 68.9 %copy-start.7 = (f32[16,24]{0,1:T(8,128)S(1)}, f32[16,24]{0,1:T(8,128)}, u32[]{:S(2)}) copy-start(f32[16,24]{0,1:T(8,128)} %get-tuple-element.40) | copy-start | bytes 4612
  406.3 34.9 %all-to-all-start.8 = ((f32[128,6,256]{2,1,0:T(8,128)}), f32[128,6,256]{2,1,0:T(8,128)}, u32[]{:S(2)}, u32[]{:S(2)}) async-start(f32[128,6,256]{2,1,0:T(8,128)} %copy.461), calls=%async_computation.8 | async-start | bytes 2097152 | tf_op jit(solution)/shard_map/all_to_all | solution.py:89
  442.8 11.6 %copy-start.2 = (f32[1,1,2,384,256]{4,3,2,1,0:T(8,128)S(1)}, f32[1,1,2,384,256]{4,3,2,1,0:T(8,128)}, u32[]{:S(2)}) copy-start(f32[1,1,2,384,256]{4,3,2,1,0:T(8,128)} %get-tuple-element.7) | copy-start | bytes 2359300
  442.9 11.6 %copy-start.3 = (f32[1,1,2,384,256]{4,3,2,1,0:T(8,128)S(1)}, f32[1,1,2,384,256]{4,3,2,1,0:T(8,128)}, u32[]{:S(2)}) copy-start(f32[1,1,2,384,256]{4,3,2,1,0:T(8,128)} %get-tuple-element.10) | copy-start | bytes 2359300
  450.5 8.9 %copy-start.9 = (f32[16,24]{1,0:T(8,128)S(1)}, f32[16,24]{1,0:T(8,128)}, u32[]{:S(2)}) copy-start(f32[16,24]{1,0:T(8,128)} %copy.443) | copy-start | bytes 4612
  467.3 29.5 %all-to-all-start.9 = ((f32[2,384,256]{2,0,1:T(2,128)}), f32[2,384,256]{2,0,1:T(2,128)S(1)}, u32[]{:S(2)}, u32[]{:S(2)}) async-start(f32[2,384,256]{2,0,1:T(2,128)} %copy.489), calls=%async_computation.9 | async-start | bytes 1572864 | tf_op jit(solution)/shard_map/all_to_all | solution.py:113
  476.4 83.8 %copy-start.15 = (f32[1,256]{1,0:T(1,128)S(1)}, f32[1,256]{1,0:T(1,128)}, u32[]{:S(2)}) copy-start(f32[1,256]{1,0:T(1,128)} %copy-done.14) | copy-start | bytes 3076
  476.4 83.8 %copy-start.16 = (f32[1,256]{1,0:T(1,128)S(1)}, f32[1,256]{1,0:T(1,128)}, u32[]{:S(2)}) copy-start(f32[1,256]{1,0:T(1,128)} %get-tuple-element.34) | copy-start | bytes 3076
  496.8 29.5 %all-to-all-start.10 = ((f32[2,384,256]{2,0,1:T(2,128)}), f32[2,384,256]{2,0,1:T(2,128)}, u32[]{:S(2)}, u32[]{:S(2)}) async-start(f32[2,384,256]{2,0,1:T(2,128)} %copy.491), calls=%async_computation.10 | async-start | bytes 1572864 | tf_op jit(solution)/shard_map/all_to_all | solution.py:118
  505.9 85.2 %copy-start.1 = (bf16[3,1024,256]{2,1,0:T(8,128)(2,1)S(1)}, bf16[3,1024,256]{2,1,0:T(8,128)(2,1)}, u32[]{:S(2)}) copy-start(bf16[3,1024,256]{2,1,0:T(8,128)(2,1)} %param.7) | copy-start | bytes 4718596
  534.2 24.1 %all-to-all-start.11 = ((f32[64,6,256]{2,1,0:T(8,128)}), f32[64,6,256]{2,1,0:T(8,128)}, u32[]{:S(2)}, u32[]{:S(2)}) async-start(f32[64,6,256]{2,1,0:T(8,128)} %copy.493), calls=%async_computation.11 | async-start | bytes 1048576 | tf_op jit(solution)/shard_map/all_to_all | solution.py:121
  541.7 47.7 %reduce-scatter.2.cloned.1.call-start = ((), (), s32[]{:S(2)}) async-start(), calls=%async_computation.13 | async-start | bytes 1966080 | tf_op jit(solution)/shard_map/reduce_scatter | solution.py:126
  (5 other events, 40.6 us)
Sparse Core Ops, SparseCore 0:
  563.3 26.0 reduce-scatter.1
